TPU v7x, 32 devices: a whole 2x2x4 slice. The times are simulated.
32 devices in a mesh: groups: 2 (over y), deg: 4 (over z), sub: 2 (over x), fld: 2 (over core).
Axes of the slice: x: 2, y: 2, z: 4, core: 2. Of those that a mesh axis runs over, the one named last changes fastest.
Arguments:
- coefficients: bfloat16 [32, 2, 32, 2048], P(None, None, ('groups', 'fld'), ('deg', 'sub')), parts along dimension 2, may hold values from -6 to 6
- delta: bfloat16 [32, 2, 2048, 2048], P('deg', None, None, 'sub'), may hold values from -0.125 to 0.125
- order_of: int32 [2048], replicated, may hold values from 0 to 2047, each once
- degree_of: int32 [32], replicated, may hold values from 512 to 2047
- angle_index: int32 [32, 3], P(('groups', 'fld')), parts along dimension 0, may hold values from 0 to 4095
Outputs:
- rotated: float32 [32, 2, 32, 2048], P(None, None, ('groups', 'fld'), ('deg', 'sub')), parts along dimension 2
There are 2 independent parts, one for each index of `groups`. A program takes and returns all parts, laid end to end along the dimension named above; an argument that names none is the same for every part. Nothing has to cross between parts.
All inputs are finite; a program needn't handle non-finite values.
Results may differ from a plain program's by a relative error of at most 0.004.
Values may be sent and summed in bfloat16 or wider, within the bound.
No kernel may reach another device: no remote copies, remote signals or barrier semaphores. Data moves between devices by JAX's collectives and lax.ppermute only.
A program may use at most 128 MiB of HBM per device.

v0:
```python
import math
import jax
import jax.numpy as jnp
from jax import lax
from jax.sharding import PartitionSpec as P

NM = 2048
NANG = 4096


def phase_pair(angle_index, column, orders):
    steps_int = angle_index[:, column][:, None] * orders[None, :] % NANG
    angle_val = steps_int.astype(jnp.float32) * (2.0 * math.pi / NANG)
    return (jnp.cos(angle_val), jnp.sin(angle_val))


def twist_phase(values, cosine, sine):
    cos_part = values[:, 0]
    sin_part = values[:, 1]
    return jnp.stack(
        [cosine * cos_part - sine * sin_part, sine * cos_part + cosine * sin_part], axis=1
    )


def live_mask(degrees, orders):
    limits = degrees[:, None]
    cosine_live = orders[None, :] <= limits
    sine_live = cosine_live & (orders[None, :] >= 1)
    return jnp.stack([cosine_live, sine_live], axis=1)[:, :, None, :].astype(jnp.float32)


def per_device(coefficients, delta, order_of, degree_of, angle_index):
    deg_size = lax.axis_size("deg")
    sub_size = lax.axis_size("sub")
    deg_count = delta.shape[0]
    col_count = delta.shape[3]
    slot_count = coefficients.shape[3]
    slot_ids = jnp.arange(NM, dtype=jnp.int32)
    inverse = jnp.zeros((NM,), jnp.int32).at[order_of].set(slot_ids)
    widened = lax.all_gather(coefficients, "sub", axis=3, tiled=True)
    slot_rows = lax.all_to_all(widened, "deg", split_axis=0, concat_axis=3, tiled=True)
    natural = jnp.take(slot_rows, inverse, axis=3)
    my_degrees = lax.dynamic_slice_in_dim(degree_of, lax.axis_index("deg") * deg_count, deg_count)
    gamma_cos, gamma_sin = phase_pair(angle_index, 2, slot_ids)
    first_turn = twist_phase(
        live_mask(my_degrees, slot_ids) * natural.astype(jnp.float32), gamma_cos, gamma_sin
    ).astype(jnp.bfloat16)
    product = jnp.einsum("kpfm,kpmn->kpfn", first_turn, delta, preferred_element_type=jnp.float32)
    col_orders = lax.axis_index("sub") * col_count + jnp.arange(col_count, dtype=jnp.int32)
    col_live = live_mask(my_degrees, col_orders)
    beta_cos, beta_sin = phase_pair(angle_index, 1, col_orders)
    middle = twist_phase(col_live * product, beta_cos, beta_sin).astype(jnp.bfloat16)
    second = jnp.einsum(
        "kpfm,kpmn->kpfn",
        lax.all_gather(middle, "sub", axis=3, tiled=True),
        delta,
        preferred_element_type=jnp.float32,
    )
    alpha_cos, alpha_sin = phase_pair(angle_index, 0, col_orders)
    result = twist_phase(col_live * second, alpha_cos, alpha_sin)
    full_cols = lax.all_gather(result, "sub", axis=3, tiled=True)
    slot_table = order_of.reshape(deg_size, sub_size, slot_count)
    pick_slots = lax.dynamic_index_in_dim(
        slot_table, lax.axis_index("sub"), 1, keepdims=False
    ).reshape(-1)
    picked = jnp.take(full_cols, pick_slots, axis=3)
    gathered = lax.all_to_all(picked, "deg", split_axis=3, concat_axis=0, tiled=True)
    return gathered


def solution(mesh):
    in_specs = (
        P(None, None, ("groups", "fld"), ("deg", "sub")),
        P("deg", None, None, "sub"),
        P(),
        P(),
        P(("groups", "fld"), None),
    )
    out_specs = P(None, None, ("groups", "fld"), ("deg", "sub"))
    return jax.shard_map(
        per_device, mesh=mesh, in_specs=in_specs, out_specs=out_specs, check_vma=False
    )
```

profile of v0, /device:TPU:0, one launch (start us, length us, event | category | flops | bytes accessed | tf_op | source)
XLA Modules:
  0.0 229.7 jit_solution(14669175599531877620)
XLA Ops:
  6.5 11.9 %all_gather.9 = bf16[32,2,8,512]{3,2,1,0:T(8,128)(2,1)} all-gather(bf16[32,2,8,256]{3,2,1,0:T(8,128)(2,1)} %param.5), channel_id=1, replica_groups=mesh['groups'=2,'deg'=4,'sub'=2,'fld'=2] {'sub'}, dimensions={3}, use_global_device_ids=true | all-gather | bytes 786432 | tf_op jit(solution)/shard_map/all_gather | solution.py:40
  18.4 4.9 %all-to-all-start = ((bf16[32,2,8,512]{3,2,1,0:T(8,128)(2,1)}), bf16[32,2,8,512]{3,2,1,0:T(8,128)(2,1)S(1)}, u32[]{:S(2)}, u32[]{:S(2)}) async-start(bf16[32,2,8,512]{3,2,1,0:T(8,128)(2,1)} %all_gather.9), calls=%async_computation | async-start | bytes 1048576 | tf_op jit(solution)/shard_map/all_to_all | solution.py:41
  23.3 0.0 all-gather.2.cloned.1.call-start
  23.3 0.7 compare_select_fusion.2
  24.0 8.0 %scatter_custom_fusion = s32[2048]{0:T(1024)S(1)} fusion(s32[2048]{0:T(1024)S(1)} %compare_select_fusion.2, s32[2048]{0:T(1024)S(1)} %iota.33, s32[]{:T(128)} %constant.69.clone.1), kind=kCustom, calls=%fused_computation.63 | custom fusion | bytes 8196 | tf_op jit(solution)/shard_map/scatter | solution.py:39
  32.1 0.8 slice_bitcast_fusion.2
  32.9 0.7 dynamic_slice.8
  33.7 0.2 iota_compare_fusion
  33.8 0.1 broadcast_compare_fusion
  33.9 0.2 add_convert_fusion.2
  34.1 0.1 copy.12
  34.2 0.3 fusion.20
  34.5 0.3 fusion.16
  34.9 2.3 %all-to-all-done = bf16[32,2,8,512]{3,2,1,0:T(8,128)(2,1)S(1)} async-done(((bf16[32,2,8,512]{3,2,1,0:T(8,128)(2,1)}), bf16[32,2,8,512]{3,2,1,0:T(8,128)(2,1)S(1)}, u32[]{:S(2)}, u32[]{:S(2)}) %all-to-all-start) | async-done | bytes 524320 | tf_op jit(solution)/shard_map/all_to_all | solution.py:41
  37.2 0.4 copy.20
  37.6 6.4 %copy.18 = bf16[8,2,8,4,512]{2,0,4,3,1:T(8,128)(2,1)} copy(bf16[8,2,8,4,512]{4,3,2,1,0:T(4,128)(2,1)S(1)} %bitcast.33) | data formatting | bytes 1048576 | tf_op jit(solution)/shard_map/all_to_all | solution.py:41
  44.0 19.9 %gather_fusion = bf16[2048,8,2,8]{3,1,2,0:T(8,128)(2,1)} fusion(bf16[8,2,8,2048]{2,0,3,1:T(8,128)(2,1)} %bitcast.32, s32[2048]{0:T(1024)S(1)} %fusion.21), kind=kCustom, calls=%fused_computation | custom fusion | bytes 1056768 | tf_op jit(solution)/shard_map/jit(_take)/gather | solution.py:42
  63.9 8.3 %copy.15 = bf16[2048,8,2,8]{0,3,2,1:T(8,128)(2,1)S(1)} copy(bf16[2048,8,2,8]{3,1,2,0:T(8,128)(2,1)} %gather_fusion) | data formatting | bytes 1048576 | tf_op jit(solution)/shard_map/jit(_take)/gather | solution.py:42
  72.2 0.1 bitcast_multiply_fusion
  72.3 0.1 subtract_convert_fusion
  72.5 22.6 %convolution_multiply_fusion.1 = f32[8,2,8,1024]{3,2,1,0:T(8,128)S(1)} fusion(bf16[8,2,2048,1024]{3,2,1,0:T(8,128)(2,1)} %param.6, bf16[8,1,8,2048]{3,2,1,0:T(8,128)(2,1)S(1)} %get-tuple-element.6, bf16[8,1,8,2048]{3,2,1,0:T(8,128)(2,1)S(1)} %get-tuple-element.5, f32[8,2,1024]{2,1,0:T(2,128)S(1)} %copy.12), kind=kOutput, calls=%fused_computation.5 | convolution fusion | flops 537264128 | bytes 68222976 | tf_op jit(solution)/shard_map/kpfm,kpmn->kpfn/dot_general | solution.py:48
  95.1 0.1 subtract_convert_fusion.1
  95.2 8.2 %all_gather.10 = bf16[8,2,8,2048]{3,2,1,0:T(8,128)(2,1)S(1)} all-gather(bf16[8,2,8,1024]{3,2,1,0:T(8,128)(2,1)S(1)} %pad_maximum_fusion.1), channel_id=1, replica_groups=mesh['groups'=2,'deg'=4,'sub'=2,'fld'=2] {'sub'}, dimensions={3}, use_global_device_ids=true | all-gather | bytes 786432 | tf_op jit(solution)/shard_map/all_gather | solution.py:55
  103.4 0.0 copy-start
  103.4 22.6 %convolution_multiply_fusion = f32[8,2,8,1024]{3,2,1,0:T(8,128)S(1)} fusion(bf16[8,2,8,2048]{3,2,1,0:T(8,128)(2,1)S(1)} %all_gather.10, bf16[8,2,2048,1024]{3,2,1,0:T(8,128)(2,1)} %param.6, f32[8,2,1024]{2,1,0:T(2,128)S(1)} %copy.12), kind=kOutput, calls=%fused_computation.4 | convolution fusion | flops 537001984 | bytes 68222976 | tf_op jit(solution)/shard_map/kpfm,kpmn->kpfn/dot_general | solution.py:53
  126.0 0.1 multiply_subtract_fusion
  126.1 0.8 pad_maximum_fusion
  126.9 0.0 all-gather.2.cloned.1.call-update
  127.0 0.0 copy-done
  127.0 19.1 %all-gather.2.cloned.1.call-done = f32[8,2,8,2048]{3,2,1,0:T(8,128)} async-done(((f32[8,2,8,1024]{3,2,1,0:T(8,128)}), f32[8,2,8,2048]{3,2,1,0:T(8,128)}) %all-gather.2.cloned.1.call-update) | async-done | bytes 1048592 | tf_op jit(solution)/shard_map/all_gather | solution.py:61
  146.2 9.7 %copy.16 = f32[8,2,8,2048]{2,0,3,1:T(8,128)} copy(f32[8,2,8,2048]{3,2,1,0:T(8,128)} %all-gather.2.cloned.1.call-done) | data formatting | bytes 2097152 | tf_op jit(solution)/shard_map/all_gather | solution.py:61
  155.9 15.4 %gather_fusion.1 = f32[1024,8,2,8]{3,1,2,0:T(8,128)} fusion(f32[8,2,8,2048]{2,0,3,1:T(8,128)} %copy.16, s32[1024]{0:T(1024)S(1)} %broadcast_clamp_fusion), kind=kCustom, calls=%fused_computation.1 | custom fusion | bytes 1052672 | tf_op jit(solution)/shard_map/jit(_take)/gather | solution.py:66
  171.3 8.7 %fusion.25 = f32[1024,2,8,8]{3,2,1,0:T(8,128)} fusion(f32[1024,8,2,8]{3,1,2,0:T(8,128)} %gather_fusion.1, pred[1024]{0:T(1024)(128)(4,1)S(1)} %compare_and_fusion.1), kind=kLoop, calls=%fused_computation.74 | loop fusion | flops 131072 | bytes 1049600
  180.0 6.6 %reshape.470 = f32[4,1,32768]{2,1,0:T(1,128)S(1)} reshape(f32[1024,2,8,8]{3,2,1,0:T(8,128)} %fusion.25) | data formatting | bytes 1048576
  186.6 18.7 %all_to_all.36 = f32[4,1,32768]{2,1,0:T(1,128)S(1)} all-to-all(f32[4,1,32768]{2,1,0:T(1,128)S(1)} %reshape.470), channel_id=1, replica_groups=mesh['groups'=2,'deg'=4,'sub'=2,'fld'=2] {'deg'}, dimensions={0} | all-to-all | bytes 1048576 | tf_op jit(solution)/shard_map/all_to_all | solution.py:67
  205.3 0.5 broadcast.453
  205.9 2.1 reduce
  208.0 7.9 %reshape.471 = f32[1024,2,8,8]{3,2,1,0:T(8,128)} reshape(f32[4,32768]{1,0:T(4,128)S(1)} %reduce) | data formatting | bytes 1048576
  215.9 6.9 %copy.17 = f32[4,8,2,8,256]{4,3,2,1,0:T(8,128)} copy(f32[4,8,2,8,256]{3,1,2,4,0:T(8,128)} %bitcast.31) | data formatting | bytes 1048576 | tf_op jit(solution)/shard_map/all_to_all | solution.py:67
  (13 shorter events, 0.1 us)
Async XLA Ops:
  18.4 18.8 %all-to-all-start = ((bf16[32,2,8,512]{3,2,1,0:T(8,128)(2,1)}), bf16[32,2,8,512]{3,2,1,0:T(8,128)(2,1)S(1)}, u32[]{:S(2)}, u32[]{:S(2)}) async-start(bf16[32,2,8,512]{3,2,1,0:T(8,128)(2,1)} %all_gather.9), calls=%async_computation | async-start | bytes 1048576 | tf_op jit(solution)/shard_map/all_to_all | solution.py:41
  23.3 122.9 %all-gather.2.cloned.1.call-start = ((), (), s32[]{:S(2)}) async-start(), calls=%async_computation.2 | async-start | bytes 1572864 | tf_op jit(solution)/shard_map/all_gather | solution.py:61
  103.4 23.6 %copy-start = (s32[2048]{0:T(1024)S(1)}, s32[2048]{0:T(1024)}, u32[]{:S(2)}) copy-start(s32[2048]{0:T(1024)} %param.7) | copy-start | bytes 24580
Sparse Core Ops, SparseCore 0:
  127.1 19.0 all-gather.1
where the time goes:
time: 231 us; the launch traced here: 230 us
  local copies, waits for them, and re-layouts  91.7 us (40%)
  matrix products  45.3 us (20%)
  blocking collectives  38.8 us (17%)
  waiting for transfers between devices  21.5 us (9%)
  other arithmetic  14 us (6%)
  between operations  13.6 us (6%)
  starting transfers between devices  4.87 us (2%)
    gather x2, local copies, waits for them, and re-layouts, per_device(): natural = jnp.take(slot_rows, inverse, axis=3)  28.2 us
    dot_general x1, matrix products, per_device(): jnp.einsum('kpfm,kpmn->kpfn', lax.all_gather(middle, 'sub', axis=3, tiled...  22.6 us
    dot_general x1, matrix products, per_device(): jnp.einsum('kpfm,kpmn->kpfn', first_turn, delta, preferred_element_type=j...  22.6 us
    all_gather x1, waiting for transfers between devices, per_device(): full_cols = lax.all_gather(result, 'sub', axis=3, tiled=True)  19.1 us
    all_to_all x1, blocking collectives, per_device(): lax.all_to_all(picked, 'deg', split_axis=3, concat_axis=0, tiled=True)  18.7 us
    gather x1, local copies, waits for them, and re-layouts, per_device(): picked = jnp.take(full_cols, pick_slots, axis=3)  15.4 us
    unnamed x4, local copies, waits for them, and re-layouts  14.5 us
    all_gather x1, blocking collectives, per_device(): widened = lax.all_gather(coefficients, 'sub', axis=3, tiled=True)  11.9 us
  transfers between devices with their start and end apart: 2, of which 2 were waited for; matrix products, arithmetic and copies ran while one was open for 5% of the time, Pallas kernels for 0%

commit v1 on v0

--- a/solution.py
+++ b/solution.py
@@ -30,6 +30,11 @@
 
 
 def per_device(coefficients, delta, order_of, degree_of, angle_index):
+
+    def _shape_column(load, comm_axis):
+        x_next = jnp.concatenate(lax.all_gather(load, comm_axis), axis=3)
+        return x_next
+
     deg_size = lax.axis_size("deg")
     sub_size = lax.axis_size("sub")
     deg_count = delta.shape[0]
@@ -58,7 +63,7 @@
     )
     alpha_cos, alpha_sin = phase_pair(angle_index, 0, col_orders)
     result = twist_phase(col_live * second, alpha_cos, alpha_sin)
-    full_cols = lax.all_gather(result, "sub", axis=3, tiled=True)
+    full_cols = _shape_column(result, "sub")
     slot_table = order_of.reshape(deg_size, sub_size, slot_count)
     pick_slots = lax.dynamic_index_in_dim(
         slot_table, lax.axis_index("sub"), 1, keepdims=False

time: 231 us -> 230 us (level)
    reshape x0 -> x1, local copies, waits for them, and re-layouts: none -> 8.47 us  [_shape_column(): x_next = jnp.concatenate(lax.all_gather(load, comm_axis), axis=3)]
    all_gather x1, local copies, waits for them, and re-layouts: 9.75 us -> 2.04 us  [_shape_column(): x_next = jnp.concatenate(lax.all_gather(load, comm_axis), axis=3)]
    all_to_all x2 -> x3, local copies, waits for them, and re-layouts: 7.43 us -> 6.64 us  [per_device(): lax.all_to_all(picked, 'deg', split_axis=3, concat_axis=0, tiled=True)]
where the time goes in v1:
time: 230 us
  local copies, waits for them, and re-layouts  91.7 us (40%)
  matrix products  45.3 us (20%)
  blocking collectives  38.8 us (17%)
  waiting for transfers between devices  21.5 us (9%)
  other arithmetic  14 us (6%)
  between operations  13.6 us (6%)
  starting transfers between devices  4.87 us (2%)
    gather x2, local copies, waits for them, and re-layouts, per_device(): natural = jnp.take(slot_rows, inverse, axis=3)  28.2 us
    dot_general x1, matrix products, per_device(): jnp.einsum('kpfm,kpmn->kpfn', lax.all_gather(middle, 'sub', axis=3, tiled...  22.6 us
    dot_general x1, matrix products, per_device(): jnp.einsum('kpfm,kpmn->kpfn', first_turn, delta, preferred_element_type=j...  22.6 us
    all_gather x1, waiting for transfers between devices, _shape_column(): x_next = jnp.concatenate(lax.all_gather(load, comm_axis), axis=3)  19.1 us
    all_to_all x1, blocking collectives, per_device(): lax.all_to_all(picked, 'deg', split_axis=3, concat_axis=0, tiled=True)  18.7 us
    gather x1, local copies, waits for them, and re-layouts, per_device(): picked = jnp.take(full_cols, pick_slots, axis=3)  15.4 us
    unnamed x4, local copies, waits for them, and re-layouts  14.5 us
    all_gather x1, blocking collectives, per_device(): widened = lax.all_gather(coefficients, 'sub', axis=3, tiled=True)  11.9 us
  transfers between devices with their start and end apart: 2, of which 2 were waited for; matrix products, arithmetic and copies ran while one was open for 5% of the time, Pallas kernels for 0%

profile of v1, /device:TPU:0, one launch (start us, length us, event | category | flops | bytes accessed | tf_op | source)
XLA Modules:
  0.0 229.7 jit_solution(11736378691079202638)
XLA Ops:
  6.5 11.9 %all_gather.12 = bf16[32,2,8,512]{3,2,1,0:T(8,128)(2,1)} all-gather(bf16[32,2,8,256]{3,2,1,0:T(8,128)(2,1)} %param.5), channel_id=1, replica_groups=mesh['groups'=2,'deg'=4,'sub'=2,'fld'=2] {'sub'}, dimensions={3}, use_global_device_ids=true | all-gather | bytes 786432 | tf_op jit(solution)/shard_map/all_gather | solution.py:45
  18.4 4.9 %all-to-all-start = ((bf16[32,2,8,512]{3,2,1,0:T(8,128)(2,1)}), bf16[32,2,8,512]{3,2,1,0:T(8,128)(2,1)S(1)}, u32[]{:S(2)}, u32[]{:S(2)}) async-start(bf16[32,2,8,512]{3,2,1,0:T(8,128)(2,1)} %all_gather.12), calls=%async_computation | async-start | bytes 1048576 | tf_op jit(solution)/shard_map/all_to_all | solution.py:46
  23.3 0.0 all-gather.3.cloned.1.call-start
  23.3 0.7 compare_select_fusion.2
  24.0 8.0 %scatter_custom_fusion = s32[2048]{0:T(1024)S(1)} fusion(s32[2048]{0:T(1024)S(1)} %compare_select_fusion.2, s32[2048]{0:T(1024)S(1)} %iota.33, s32[]{:T(128)} %constant.69.clone.1), kind=kCustom, calls=%fused_computation.64 | custom fusion | bytes 8196 | tf_op jit(solution)/shard_map/scatter | solution.py:44
  32.1 0.8 slice_bitcast_fusion.2
  32.9 0.7 dynamic_slice.8
  33.7 0.2 iota_compare_fusion
  33.8 0.1 broadcast_compare_fusion
  33.9 0.2 add_convert_fusion.2
  34.1 0.1 copy.26
  34.2 0.3 fusion.20
  34.5 0.3 fusion.16
  34.9 2.3 %all-to-all-done = bf16[32,2,8,512]{3,2,1,0:T(8,128)(2,1)S(1)} async-done(((bf16[32,2,8,512]{3,2,1,0:T(8,128)(2,1)}), bf16[32,2,8,512]{3,2,1,0:T(8,128)(2,1)S(1)}, u32[]{:S(2)}, u32[]{:S(2)}) %all-to-all-start) | async-done | bytes 524320 | tf_op jit(solution)/shard_map/all_to_all | solution.py:46
  37.2 0.4 copy.40
  37.6 6.4 %copy.34 = bf16[8,2,8,4,512]{2,0,4,3,1:T(8,128)(2,1)} copy(bf16[8,2,8,4,512]{4,3,2,1,0:T(4,128)(2,1)S(1)} %bitcast.39) | data formatting | bytes 1048576 | tf_op jit(solution)/shard_map/all_to_all | solution.py:46
  44.0 19.9 %gather_fusion = bf16[2048,8,2,8]{3,1,2,0:T(8,128)(2,1)} fusion(bf16[8,2,8,2048]{2,0,3,1:T(8,128)(2,1)} %bitcast.37, s32[2048]{0:T(1024)S(1)} %fusion.21), kind=kCustom, calls=%fused_computation | custom fusion | bytes 1056768 | tf_op jit(solution)/shard_map/jit(_take)/gather | solution.py:47
  63.9 8.3 %copy.29 = bf16[2048,8,2,8]{0,3,2,1:T(8,128)(2,1)S(1)} copy(bf16[2048,8,2,8]{3,1,2,0:T(8,128)(2,1)} %gather_fusion) | data formatting | bytes 1048576 | tf_op jit(solution)/shard_map/jit(_take)/gather | solution.py:47
  72.2 0.1 bitcast_multiply_fusion
  72.3 0.1 subtract_convert_fusion
  72.5 22.6 %convolution_multiply_fusion.1 = f32[8,2,8,1024]{3,2,1,0:T(8,128)S(1)} fusion(bf16[8,2,2048,1024]{3,2,1,0:T(8,128)(2,1)} %param.6, bf16[8,1,8,2048]{3,2,1,0:T(8,128)(2,1)S(1)} %get-tuple-element.6, bf16[8,1,8,2048]{3,2,1,0:T(8,128)(2,1)S(1)} %get-tuple-element.5, f32[8,2,1024]{2,1,0:T(2,128)S(1)} %copy.26), kind=kOutput, calls=%fused_computation.5 | convolution fusion | flops 537264128 | bytes 68222976 | tf_op jit(solution)/shard_map/kpfm,kpmn->kpfn/dot_general | solution.py:53
  95.1 0.1 subtract_convert_fusion.1
  95.2 8.2 %all_gather.13 = bf16[8,2,8,2048]{3,2,1,0:T(8,128)(2,1)S(1)} all-gather(bf16[8,2,8,1024]{3,2,1,0:T(8,128)(2,1)S(1)} %pad_maximum_fusion.1), channel_id=1, replica_groups=mesh['groups'=2,'deg'=4,'sub'=2,'fld'=2] {'sub'}, dimensions={3}, use_global_device_ids=true | all-gather | bytes 786432 | tf_op jit(solution)/shard_map/all_gather | solution.py:60
  103.4 0.0 copy-start
  103.4 22.6 %convolution_multiply_fusion = f32[8,2,8,1024]{3,2,1,0:T(8,128)S(1)} fusion(bf16[8,2,8,2048]{3,2,1,0:T(8,128)(2,1)S(1)} %all_gather.13, bf16[8,2,2048,1024]{3,2,1,0:T(8,128)(2,1)} %param.6, f32[8,2,1024]{2,1,0:T(2,128)S(1)} %copy.26), kind=kOutput, calls=%fused_computation.4 | convolution fusion | flops 537001984 | bytes 68222976 | tf_op jit(solution)/shard_map/kpfm,kpmn->kpfn/dot_general | solution.py:58
  126.0 0.1 multiply_subtract_fusion
  126.1 0.8 pad_maximum_fusion
  126.9 0.0 all-gather.3.cloned.1.call-update
  127.0 0.0 copy-done
  127.0 19.1 %all-gather.3.cloned.1.call-done = f32[16,2,8,1024]{3,2,1,0:T(8,128)} async-done(((f32[8,2,8,1024]{3,2,1,0:T(8,128)}), f32[16,2,8,1024]{3,2,1,0:T(8,128)}) %all-gather.3.cloned.1.call-update) | async-done | bytes 1048592 | tf_op jit(solution)/shard_map/all_gather | solution.py:35
  146.2 2.0 copy.39
  148.2 8.5 %copy.35 = f32[8,2,8,2,1024]{2,0,4,3,1:T(8,128)} copy(f32[8,2,8,2,1024]{4,3,2,1,0:T(2,128)S(1)} %bitcast.38) | data formatting | bytes 2097152 | tf_op jit(solution)/shard_map/reshape | solution.py:35
  156.7 15.4 %gather_fusion.1 = f32[1024,8,2,8]{3,1,2,0:T(8,128)} fusion(f32[8,2,8,2048]{2,0,3,1:T(8,128)} %bitcast.36, s32[1024]{0:T(1024)S(1)} %broadcast_clamp_fusion), kind=kCustom, calls=%fused_computation.1 | custom fusion | bytes 1052672 | tf_op jit(solution)/shard_map/jit(_take)/gather | solution.py:71
  172.1 8.7 %fusion.25 = f32[1024,2,8,8]{3,2,1,0:T(8,128)} fusion(f32[1024,8,2,8]{3,1,2,0:T(8,128)} %gather_fusion.1, pred[1024]{0:T(1024)(128)(4,1)S(1)} %compare_and_fusion.1), kind=kLoop, calls=%fused_computation.75 | loop fusion | flops 131072 | bytes 1049600
  180.8 6.6 %reshape.479 = f32[4,1,32768]{2,1,0:T(1,128)S(1)} reshape(f32[1024,2,8,8]{3,2,1,0:T(8,128)} %fusion.25) | data formatting | bytes 1048576
  187.4 18.7 %all_to_all.36 = f32[4,1,32768]{2,1,0:T(1,128)S(1)} all-to-all(f32[4,1,32768]{2,1,0:T(1,128)S(1)} %reshape.479), channel_id=1, replica_groups=mesh['groups'=2,'deg'=4,'sub'=2,'fld'=2] {'deg'}, dimensions={0} | all-to-all | bytes 1048576 | tf_op jit(solution)/shard_map/all_to_all | solution.py:72
  206.1 0.5 broadcast.453
  206.6 2.1 reduce
  208.8 7.9 %reshape.480 = f32[1024,2,8,8]{3,2,1,0:T(8,128)} reshape(f32[4,32768]{1,0:T(4,128)S(1)} %reduce) | data formatting | bytes 1048576
  216.7 5.2 %copy.36 = f32[8,2,8,4,256]{4,3,2,1,0:T(4,128)S(1)} copy(f32[8,2,8,4,256]{2,0,1,4,3:T(8,128)} %bitcast.35) | data formatting | bytes 1048576 | tf_op jit(solution)/shard_map/all_to_all | solution.py:72
  221.9 0.9 copy.33
  (13 shorter events, 0.1 us)
Async XLA Ops:
  18.4 18.8 %all-to-all-start = ((bf16[32,2,8,512]{3,2,1,0:T(8,128)(2,1)}), bf16[32,2,8,512]{3,2,1,0:T(8,128)(2,1)S(1)}, u32[]{:S(2)}, u32[]{:S(2)}) async-start(bf16[32,2,8,512]{3,2,1,0:T(8,128)(2,1)} %all_gather.12), calls=%async_computation | async-start | bytes 1048576 | tf_op jit(solution)/shard_map/all_to_all | solution.py:46
  23.3 122.9 %all-gather.3.cloned.1.call-start = ((), (), s32[]{:S(2)}) async-start(), calls=%async_computation.2 | async-start | bytes 1572864 | tf_op jit(solution)/shard_map/all_gather | solution.py:35
  103.4 23.6 %copy-start = (s32[2048]{0:T(1024)S(1)}, s32[2048]{0:T(1024)}, u32[]{:S(2)}) copy-start(s32[2048]{0:T(1024)} %param.7) | copy-start | bytes 24580
Sparse Core Ops, SparseCore 0:
  127.1 19.0 all-gather.2
